TPU v7x, 32 devices: a whole 2x2x4 slice. The times are simulated.
32 devices in a mesh: groups: 2 (over y), arow: 16 (over z, x, core).
Axes of the slice: x: 2, y: 2, z: 4, core: 2. Of those that a mesh axis runs over, the one named last changes fastest.
Arguments:
- feat_a: bfloat16 [64, 32, 256], P(('groups', 'arow')), parts along dimension 0, may hold values from -6 to 6
- feat_b: bfloat16 [32, 32, 256], P(('groups', 'arow')), parts along dimension 0, may hold values from -6 to 6
- a_first: float32 [8, 3, 3], replicated, may hold values from -2 to 2
- b_first: float32 [8, 3, 3], replicated, may hold values from -2 to 2
- bias_first: float32 [8], replicated, may hold values from -3 to 3
- a_second: float32 [8, 3, 3], replicated, may hold values from -1.5 to 1.5
- b_second: float32 [8, 3, 3], replicated, may hold values from -1.5 to 1.5
- bias_second: float32 [1], replicated, may hold values from -3 to 3
Outputs:
- matches: float32 [64, 32, 512], P(('groups', 'arow')), parts along dimension 0
There are 2 independent parts, one for each index of `groups`. A program takes and returns all parts, laid end to end along the dimension named above; an argument that names none is the same for every part. Nothing has to cross between parts.
All inputs are finite; a program needn't handle non-finite values.
Results may differ from a plain program's by a relative error of at most 0.0081.
Values may be sent and summed in bfloat16 or wider, within the bound.
No kernel may reach another device: no remote copies, remote signals or barrier semaphores. Data moves between devices by JAX's collectives and lax.ppermute only.
A program may use at most 128 MiB of HBM per device.

v0:
```python
import jax
import jax.numpy as jnp
from jax import lax
from jax.sharding import PartitionSpec as P

EPSILON = 1e-05


def padded(cells, sides, width):
    for axis, dim in sides:
        count = lax.axis_size(axis)
        ends = count - 1
        head = lax.slice_in_dim(cells, 0, width, axis=dim)
        tail = lax.slice_in_dim(cells, cells.shape[dim] - width, cells.shape[dim], axis=dim)
        cells = jnp.concatenate(
            [
                lax.ppermute(tail, axis, [(i, (i + 1) % count) for i in range(ends)]),
                cells,
                lax.ppermute(head, axis, [((i + 1) % count, i) for i in range(ends)]),
            ],
            axis=dim,
        )
    return cells


def shifted_zero(values, along, offset):
    extent = values.shape[along]
    if offset == 0:
        return values
    widths = [(0, 0)] * values.ndim
    if offset > 0:
        widths[along] = (0, offset)
        return lax.slice_in_dim(jnp.pad(values, widths), offset, offset + extent, axis=along)
    widths[along] = (-offset, 0)
    return lax.slice_in_dim(jnp.pad(values, widths), 0, extent, axis=along)


def conv_a(values, kernel):
    out_rows = values.shape[-3] - 2
    result = 0.0
    for row_tap in range(3):
        row_slab = lax.slice_in_dim(
            values, row_tap, row_tap + out_rows, axis=values.ndim - 3
        ).astype(jnp.float32)
        for col_tap in range(3):
            result = result + kernel[..., row_tap, col_tap][..., None, None, None] * shifted_zero(
                row_slab, values.ndim - 2, col_tap - 1
            )
    return result


def conv_b(values, kernel, map_width):
    flat_pos = lax.broadcasted_iota(jnp.int32, (values.shape[-1],), 0) % map_width
    result = 0.0
    for row_tap in range(3):
        for col_tap in range(3):
            shifted = shifted_zero(
                values, values.ndim - 1, (row_tap - 1) * map_width + (col_tap - 1)
            )
            inside = ((flat_pos + col_tap - 1 >= 0) & (flat_pos + col_tap - 1 < map_width)).astype(
                jnp.float32
            )
            result = result + kernel[..., row_tap, col_tap][..., None, None, None] * (
                shifted * inside
            )
    return result


def first_layer(correlation, kern_a, kern_b, bias_one, map_width):
    spread = conv_a(correlation, kern_a)
    return jax.nn.relu(conv_b(spread, kern_b, map_width) + bias_one[:, None, None, None]).astype(
        jnp.bfloat16
    )


def second_layer(hidden, kern_a, kern_b, bias_two, map_width):
    spread = conv_a(hidden, kern_a)
    summed = jnp.sum(conv_b(spread, kern_b, map_width), axis=0)
    return jax.nn.relu(summed + bias_two[0])


def on_device(feat_a, feat_b, a_first, b_first, bias_first, a_second, b_second, bias_second):
    map_width = feat_b.shape[1]
    channels = feat_a.shape[2]
    b_cells = feat_b.shape[0] * lax.axis_size("arow") * map_width
    a_rows = feat_a.reshape(-1, channels)
    tile_product = lax.dot_general(
        a_rows,
        lax.all_gather(feat_b, "arow", axis=0, tiled=True).reshape(-1, channels),
        (((1,), (1,)), ((), ())),
        preferred_element_type=jnp.float32,
    )
    correlation = (
        (tile_product * channels ** (-0.5))
        .astype(jnp.bfloat16)
        .reshape(feat_a.shape[0], map_width, b_cells)
    )
    correlation = padded(correlation, (("arow", 0),), 1)

    def network(kern_a1, kern_b1, kern_a2, kern_b2):
        hidden = first_layer(correlation, kern_a1, kern_b1, bias_first, map_width)
        hidden = padded(hidden, (("arow", 1),), 1)
        return second_layer(hidden, kern_a2, kern_b2, bias_second, map_width)

    score = network(a_first, b_first, a_second, b_second)
    score = score + network(b_first, a_first, b_second, a_second)
    best_over_a = lax.pmax(jnp.max(score, axis=(0, 1)), "arow")
    best_over_b = jnp.max(score, axis=2)[..., None]
    return score * (score / (best_over_a + EPSILON)) * (score / (best_over_b + EPSILON))


def solution(mesh):
    return jax.shard_map(
        on_device,
        mesh=mesh,
        in_specs=(
            P(("groups", "arow"), None, None),
            P(("groups", "arow"), None, None),
            P(),
            P(),
            P(),
            P(),
            P(),
            P(),
        ),
        out_specs=P(("groups", "arow"), None, None),
        check_vma=False,
    )
```

profile of v0, /device:TPU:0, one launch (start us, length us, event | category | flops | bytes accessed | tf_op | source)
XLA Modules:
  0.0 88.3 jit_solution(9698802883479565245)
XLA Ops:
  0.0 0.0 copy-start
  0.0 24.2 %all_gather.3 = bf16[16,32,256]{2,1,0:T(8,128)(2,1)S(1)} all-gather(bf16[1,32,256]{2,1,0:T(8,128)(2,1)} %param.9), channel_id=1, replica_groups=mesh['groups'=2,'arow'=16] {'arow'}, dimensions={0}, use_global_device_ids=true | all-gather | bytes 278528 | tf_op jit(solution)/shard_map/all_gather | solution.py:89
  24.2 0.2 fusion
  24.4 2.3 %collective-permute-start = (bf16[1,32,512]{2,1,0:T(8,128)(2,1)S(1)}, bf16[1,32,512]{2,1,0:T(8,128)(2,1)S(1)}, u32[]{:S(2)}, u32[]{:S(2)}) collective-permute-start(bf16[1,32,512]{2,1,0:T(8,128)(2,1)S(1)} %get-tuple-element.28), channel_id=1, source_target_pairs={{0,1},{1,2},{2,3},{3,4},{4,5},{5,6},{6,7},{7,8},{8,9},{9,10},{10,1... | collective-permute-start | bytes 98312 | tf_op jit(solution)/shard_map/ppermute | solution.py:17
  26.7 1.3 %collective-permute-start.1 = (bf16[1,32,512]{2,1,0:T(8,128)(2,1)S(1)}, bf16[1,32,512]{2,1,0:T(8,128)(2,1)S(1)}, u32[]{:S(2)}, u32[]{:S(2)}) collective-permute-start(bf16[1,32,512]{2,1,0:T(8,128)(2,1)S(1)} %get-tuple-element.29), channel_id=1, source_target_pairs={{1,0},{2,1},{3,2},{4,3},{5,4},{6,5},{7,6},{8,7},{9,8},{10,9},{11,1... | collective-permute-start | bytes 98312 | tf_op jit(solution)/shard_map/ppermute | solution.py:19
  28.0 0.8 slice_bitcast_fusion.34
  28.9 0.0 copy-done.3
  29.6 0.0 collective-permute-done
  29.6 0.1 collective-permute-done.1
  29.8 0.1 pad_slice_fusion.45
  29.8 0.7 multiply_add_fusion.1
  30.6 0.0 copy-start.4
  30.6 0.7 multiply_add_fusion
  31.3 2.5 %fusion.150 = (f32[8,2,32,512]{3,2,1,0:T(8,128)S(1)}, bf16[8,2,32,512]{3,2,1,0:T(8,128)(2,1)S(1)}) fusion(f32[8]{0:T(128)S(1)} %copy-done.4, f32[8,2,32,512]{3,2,1,0:T(8,128)S(1)} %multiply_add_fusion.1, f32[8]{0:T(128)S(1)} %get-tuple-element.64, f32[8]{0:T(128)S(1)} %get-tuple-element.65, f32[8]{0:T(128)S(1)} %get-tuple-element.58, ...), kind=kLoop, calls=%fused_computation.255 | loop fusion | flops 7864320 | bytes 2627904 | tf_op jit(solution)/shard_map/convert_element_type | solution.py:44
  33.8 4.1 %collective-permute-start.2 = (bf16[8,1,32,512]{3,2,1,0:T(8,128)(2,1)S(1)}, bf16[8,1,32,512]{3,2,1,0:T(8,128)(2,1)S(1)}, u32[]{:S(2)}, u32[]{:S(2)}) collective-permute-start(bf16[8,1,32,512]{3,2,1,0:T(8,128)(2,1)S(1)} %get-tuple-element.15), channel_id=1, source_target_pairs={{0,1},{1,2},{2,3},{3,4},{4,5},{5,6},{6,7},{7,8},{8,9},{9,10},{10,1... | collective-permute-start | bytes 786440 | tf_op jit(solution)/shard_map/ppermute | solution.py:17
  37.9 1.3 %collective-permute-start.3 = (bf16[8,1,32,512]{3,2,1,0:T(8,128)(2,1)S(1)}, bf16[8,1,32,512]{3,2,1,0:T(8,128)(2,1)S(1)}, u32[]{:S(2)}, u32[]{:S(2)}) collective-permute-start(bf16[8,1,32,512]{3,2,1,0:T(8,128)(2,1)S(1)} %get-tuple-element.14), channel_id=1, source_target_pairs={{1,0},{2,1},{3,2},{4,3},{5,4},{6,5},{7,6},{8,7},{9,8},{10,9},{11,1... | collective-permute-start | bytes 786440 | tf_op jit(solution)/shard_map/ppermute | solution.py:19
  39.2 2.5 %fusion.152 = (f32[8,2,32,512]{3,2,1,0:T(8,128)S(1)}, bf16[8,2,32,512]{3,2,1,0:T(8,128)(2,1)S(1)}) fusion(f32[8]{0:T(128)S(1)} %copy-done.4, f32[8,2,32,512]{3,2,1,0:T(8,128)S(1)} %multiply_add_fusion, f32[8]{0:T(128)S(1)} %get-tuple-element.55, f32[8]{0:T(128)S(1)} %get-tuple-element.56, f32[8]{0:T(128)S(1)} %get-tuple-element.49, ...), kind=kLoop, calls=%fused_computation.256 | loop fusion | flops 7864320 | bytes 2627904 | tf_op jit(solution)/shard_map/convert_element_type | solution.py:44
  41.7 3.0 %collective-permute-start.4 = (bf16[8,1,32,512]{3,2,1,0:T(8,128)(2,1)S(1)}, bf16[8,1,32,512]{3,2,1,0:T(8,128)(2,1)S(1)}, u32[]{:S(2)}, u32[]{:S(2)}) collective-permute-start(bf16[8,1,32,512]{3,2,1,0:T(8,128)(2,1)S(1)} %get-tuple-element.19), channel_id=1, source_target_pairs={{0,1},{1,2},{2,3},{3,4},{4,5},{5,6},{6,7},{7,8},{8,9},{9,10},{10,1... | collective-permute-start | bytes 786440 | tf_op jit(solution)/shard_map/ppermute | solution.py:17
  44.8 1.3 %collective-permute-start.5 = (bf16[8,1,32,512]{3,2,1,0:T(8,128)(2,1)S(1)}, bf16[8,1,32,512]{3,2,1,0:T(8,128)(2,1)S(1)}, u32[]{:S(2)}, u32[]{:S(2)}) collective-permute-start(bf16[8,1,32,512]{3,2,1,0:T(8,128)(2,1)S(1)} %get-tuple-element.18), channel_id=1, source_target_pairs={{1,0},{2,1},{3,2},{4,3},{5,4},{6,5},{7,6},{8,7},{9,8},{10,9},{11,1... | collective-permute-start | bytes 786440 | tf_op jit(solution)/shard_map/ppermute | solution.py:19
  46.1 0.0 collective-permute-done.2
  46.1 0.0 collective-permute-done.3
  46.1 0.1 fusion.135
  46.2 1.6 %fusion.35 = f32[8,2,32,512]{3,2,1,0:T(8,128)S(1)} fusion(f32[8,2,32,512]{3,2,1,0:T(8,128)S(1)} %get-tuple-element.13, f32[8,2,32,512]{3,2,1,0:T(8,128)S(1)} %get-tuple-element.8, f32[8,2,32,512]{3,2,1,0:T(8,128)S(1)} %get-tuple-element.12, f32[8]{0:T(128)S(1)} %get-tuple-element.37, f32[8]{0:T(128)S(1)} %get-tuple-element.38, f32[8]{0:T(128)S(1)} %get-tuple-element.31, ...), kind=kLoop, calls=%fused_computation.80 | loop fusion | flops 4456448 | bytes 4194592 | tf_op jit(solution)/shard_map/add | solution.py:46
  47.8 2.4 %fusion.132 = f32[2,32,512]{2,1,0:T(8,128)S(1)} fusion(f32[8,2,32,512]{3,2,1,0:T(8,128)S(1)} %fusion.35, f32[8]{0:T(128)S(1)} %get-tuple-element.46, f32[8]{0:T(128)S(1)} %get-tuple-element.47, f32[8]{0:T(128)S(1)} %get-tuple-element.40, f32[8]{0:T(128)S(1)} %get-tuple-element.41, f32[8]{0:T(128)S(1)} %get-tuple-element.42, f32[8]{0:T(128)S(1)} %get-tuple-element.43, ...), kind=kLoop, calls=%fused_computation.179 | loop fusion | flops 7045120 | bytes 1186080 | tf_op jit(solution)/shard_map/reduce_sum | solution.py:78
  50.3 0.0 collective-permute-done.4
  50.3 0.0 collective-permute-done.5
  50.3 0.1 fusion.133
  50.4 1.6 %fusion.99 = f32[8,2,32,512]{3,2,1,0:T(8,128)S(1)} fusion(f32[8,2,32,512]{3,2,1,0:T(8,128)S(1)} %get-tuple-element.17, f32[8,2,32,512]{3,2,1,0:T(8,128)S(1)} %get-tuple-element.10, f32[8,2,32,512]{3,2,1,0:T(8,128)S(1)} %get-tuple-element.16, f32[8]{0:T(128)S(1)} %get-tuple-element.46, f32[8]{0:T(128)S(1)} %get-tuple-element.47, f32[8]{0:T(128)S(1)} %get-tuple-element.40, ...), kind=kLoop, calls=%fused_computation.144 | loop fusion | flops 4456448 | bytes 4194592 | tf_op jit(solution)/shard_map/add | solution.py:46
  52.1 2.4 %fusion.131 = f32[2,32,512]{2,1,0:T(8,128)S(1)} fusion(f32[8,2,32,512]{3,2,1,0:T(8,128)S(1)} %fusion.99, f32[8]{0:T(128)S(1)} %get-tuple-element.37, f32[8]{0:T(128)S(1)} %get-tuple-element.38, f32[8]{0:T(128)S(1)} %get-tuple-element.31, f32[8]{0:T(128)S(1)} %get-tuple-element.32, f32[8]{0:T(128)S(1)} %get-tuple-element.33, f32[8]{0:T(128)S(1)} %get-tuple-element.34, ...), kind=kLoop, calls=%fused_computation.178 | loop fusion | flops 7045120 | bytes 1186080 | tf_op jit(solution)/shard_map/reduce_sum | solution.py:78
  54.5 0.1 fusion.149
  54.6 32.9 %pmax.7 = f32[512]{0:T(512)S(1)} all-reduce(f32[512]{0:T(512)S(1)} %get-tuple-element.5), channel_id=1, replica_groups=mesh['groups'=2,'arow'=16] {'arow'}, use_global_device_ids=true, to_apply=%region_3.4 | all-reduce | flops 512 | bytes 4096 | tf_op jit(solution)/shard_map/pmax | solution.py:107
  87.5 0.7 fusion.137
  (20 shorter events, 0.2 us)
Async XLA Ops:
  0.0 24.2 %copy-start = (bf16[2,32,256]{2,1,0:T(8,128)(2,1)S(1)}, bf16[2,32,256]{2,1,0:T(8,128)(2,1)}, u32[]{:S(2)}) copy-start(bf16[2,32,256]{2,1,0:T(8,128)(2,1)} %param.8) | copy-start | bytes 98308
  0.0 28.9 %copy-start.1 = (f32[8,3,3]{0,2,1:T(4,128)S(1)}, f32[8,3,3]{0,2,1:T(4,128)}, u32[]{:S(2)}) copy-start(f32[8,3,3]{0,2,1:T(4,128)} %param.11) | copy-start | bytes 868
  0.0 28.9 %copy-start.2 = (f32[8,3,3]{0,2,1:T(4,128)S(1)}, f32[8,3,3]{0,2,1:T(4,128)}, u32[]{:S(2)}) copy-start(f32[8,3,3]{0,2,1:T(4,128)} %param.13) | copy-start | bytes 868
  0.0 28.9 %copy-start.3 = (f32[8,3,3]{0,2,1:T(4,128)S(1)}, f32[8,3,3]{0,2,1:T(4,128)}, u32[]{:S(2)}) copy-start(f32[8,3,3]{0,2,1:T(4,128)} %param.14) | copy-start | bytes 868
  24.4 5.2 %collective-permute-start = (bf16[1,32,512]{2,1,0:T(8,128)(2,1)S(1)}, bf16[1,32,512]{2,1,0:T(8,128)(2,1)S(1)}, u32[]{:S(2)}, u32[]{:S(2)}) collective-permute-start(bf16[1,32,512]{2,1,0:T(8,128)(2,1)S(1)} %get-tuple-element.28), channel_id=1, source_target_pairs={{0,1},{1,2},{2,3},{3,4},{4,5},{5,6},{6,7},{7,8},{8,9},{9,10},{10,1... | collective-permute-start | bytes 98312 | tf_op jit(solution)/shard_map/ppermute | solution.py:17
  26.7 3.1 %collective-permute-start.1 = (bf16[1,32,512]{2,1,0:T(8,128)(2,1)S(1)}, bf16[1,32,512]{2,1,0:T(8,128)(2,1)S(1)}, u32[]{:S(2)}, u32[]{:S(2)}) collective-permute-start(bf16[1,32,512]{2,1,0:T(8,128)(2,1)S(1)} %get-tuple-element.29), channel_id=1, source_target_pairs={{1,0},{2,1},{3,2},{4,3},{5,4},{6,5},{7,6},{8,7},{9,8},{10,9},{11,1... | collective-permute-start | bytes 98312 | tf_op jit(solution)/shard_map/ppermute | solution.py:19
  30.6 0.7 copy-start.4
  33.8 12.2 %collective-permute-start.2 = (bf16[8,1,32,512]{3,2,1,0:T(8,128)(2,1)S(1)}, bf16[8,1,32,512]{3,2,1,0:T(8,128)(2,1)S(1)}, u32[]{:S(2)}, u32[]{:S(2)}) collective-permute-start(bf16[8,1,32,512]{3,2,1,0:T(8,128)(2,1)S(1)} %get-tuple-element.15), channel_id=1, source_target_pairs={{0,1},{1,2},{2,3},{3,4},{4,5},{5,6},{6,7},{7,8},{8,9},{9,10},{10,1... | collective-permute-start | bytes 786440 | tf_op jit(solution)/shard_map/ppermute | solution.py:17
  37.9 8.2 %collective-permute-start.3 = (bf16[8,1,32,512]{3,2,1,0:T(8,128)(2,1)S(1)}, bf16[8,1,32,512]{3,2,1,0:T(8,128)(2,1)S(1)}, u32[]{:S(2)}, u32[]{:S(2)}) collective-permute-start(bf16[8,1,32,512]{3,2,1,0:T(8,128)(2,1)S(1)} %get-tuple-element.14), channel_id=1, source_target_pairs={{1,0},{2,1},{3,2},{4,3},{5,4},{6,5},{7,6},{8,7},{9,8},{10,9},{11,1... | collective-permute-start | bytes 786440 | tf_op jit(solution)/shard_map/ppermute | solution.py:19
  41.7 8.6 %collective-permute-start.4 = (bf16[8,1,32,512]{3,2,1,0:T(8,128)(2,1)S(1)}, bf16[8,1,32,512]{3,2,1,0:T(8,128)(2,1)S(1)}, u32[]{:S(2)}, u32[]{:S(2)}) collective-permute-start(bf16[8,1,32,512]{3,2,1,0:T(8,128)(2,1)S(1)} %get-tuple-element.19), channel_id=1, source_target_pairs={{0,1},{1,2},{2,3},{3,4},{4,5},{5,6},{6,7},{7,8},{8,9},{9,10},{10,1... | collective-permute-start | bytes 786440 | tf_op jit(solution)/shard_map/ppermute | solution.py:17
  44.8 5.5 %collective-permute-start.5 = (bf16[8,1,32,512]{3,2,1,0:T(8,128)(2,1)S(1)}, bf16[8,1,32,512]{3,2,1,0:T(8,128)(2,1)S(1)}, u32[]{:S(2)}, u32[]{:S(2)}) collective-permute-start(bf16[8,1,32,512]{3,2,1,0:T(8,128)(2,1)S(1)} %get-tuple-element.18), channel_id=1, source_target_pairs={{1,0},{2,1},{3,2},{4,3},{5,4},{6,5},{7,6},{8,7},{9,8},{10,9},{11,1... | collective-permute-start | bytes 786440 | tf_op jit(solution)/shard_map/ppermute | solution.py:19
where the time goes:
time: 88.6 us; the launch traced here: 88.3 us
  blocking collectives  57.1 us (64%)
  other arithmetic  15.6 us (18%)
  starting transfers between devices  13.2 us (15%)
  local copies, waits for them, and re-layouts  1.06 us (1%)
  between operations  0.94 us (1%)
    pmax x1, blocking collectives, on_device(): best_over_a = lax.pmax(jnp.max(score, axis=(0, 1)), 'arow')  32.9 us
    all_gather x1, blocking collectives, on_device(): lax.all_gather(feat_b, 'arow', axis=0, tiled=True).reshape(-1, channels)  24.2 us
    ppermute x3, starting transfers between devices, padded(): lax.ppermute(tail, axis, [(i, (i + 1) % count) for i in range(ends)])  9.37 us
    convert_element_type x6, other arithmetic, conv_a(): row_slab = lax.slice_in_dim(values, row_tap, row_tap + out_rows, axis=val...  5.23 us
    reduce_sum x2, other arithmetic, second_layer(): summed = jnp.sum(conv_b(spread, kern_b, map_width), axis=0)  4.84 us
    add x4, other arithmetic, conv_a(): result + kernel[..., row_tap, col_tap][..., None, None, None] * shifted_z...  4.64 us
    ppermute x3, starting transfers between devices, padded(): lax.ppermute(head, axis, [((i + 1) % count, i) for i in range(ends)])  3.88 us
  transfers between devices with their start and end apart: 6, of which 1 were waited for; matrix products, arithmetic and copies ran while one was open for 9% of the time, Pallas kernels for 0%

commit v1 on v0

--- a/solution.py
+++ b/solution.py
@@ -4,6 +4,12 @@
 from jax.sharding import PartitionSpec as P
 
 EPSILON = 1e-05
+
+
+def grid_rest(x_local, axis_no):
+    arr_next = list(x_local.shape[1:])
+    arr_next[axis_no] *= x_local.shape[0]
+    return jnp.moveaxis(x_local, 0, axis_no).reshape(arr_next)
 
 
 def padded(cells, sides, width):
@@ -84,9 +90,27 @@
     channels = feat_a.shape[2]
     b_cells = feat_b.shape[0] * lax.axis_size("arow") * map_width
     a_rows = feat_a.reshape(-1, channels)
+
+    def routes_all_group(u_in, mesh_name, dim_at):
+        axis_len = lax.axis_size(mesh_name)
+        made = [(dev_j, (dev_j + 1) % axis_len) for dev_j in range(axis_len)]
+        slots = [(c, hop_no) for hop_no, c in made]
+        x_next, local_next = ([], [])
+        for w in range(axis_len - 1):
+            if w % 2 == 0:
+                x_next.append(lax.ppermute(x_next[-1] if x_next else u_in, mesh_name, made))
+            else:
+                local_next.append(
+                    lax.ppermute(local_next[-1] if local_next else u_in, mesh_name, slots)
+                )
+        current_value = jnp.stack([*x_next[::-1], u_in, *local_next], 0)
+        reply = lax.axis_index(mesh_name) - len(x_next)
+        current_value = current_value[(jnp.arange(axis_len) - reply) % axis_len]
+        return grid_rest(current_value, dim_at)
+
     tile_product = lax.dot_general(
         a_rows,
-        lax.all_gather(feat_b, "arow", axis=0, tiled=True).reshape(-1, channels),
+        routes_all_group(feat_b, "arow", 0).reshape(-1, channels),
         (((1,), (1,)), ((), ())),
         preferred_element_type=jnp.float32,
     )

time: 88.6 us -> 116 us (1.31)
  starting transfers between devices: 13.2 us -> 42.5 us
  blocking collectives: 57.1 us -> 37.1 us
  waiting for transfers between devices: 0.15 us -> 13.8 us
  local copies, waits for them, and re-layouts: 1.06 us -> 4.87 us
    ppermute x0 -> x15, starting transfers between devices: none -> 32.1 us  [the longest x7 31.6 us: routes_all_group(): lax.ppermute(local_next[-1] if local_next else u_in, mesh_name, slots)]
    all_gather x1 -> x0, blocking collectives: 24.2 us -> none  [on_device(): lax.all_gather(feat_b, 'arow', axis=0, tiled=True).reshape(-1, channels)]
    ppermute x0 -> x15, waiting for transfers between devices: none -> 12 us  [the longest x8 8.8 us: routes_all_group(): x_next.append(lax.ppermute(x_next[-1] if x_next else u_in, mesh_name, made))]
    pmax x1, blocking collectives: 32.9 us -> 37.1 us  [on_device(): best_over_a = lax.pmax(jnp.max(score, axis=(0, 1)), 'arow')]
    ppermute x3, starting transfers between devices: 9.37 us -> 6.42 us  [padded(): lax.ppermute(tail, axis, [(i, (i + 1) % count) for i in range(ends)])]
    mul x2, local copies, waits for them, and re-layouts: 0.01 us -> 1.69 us  [conv_b(): kernel[..., row_tap, col_tap][..., None, None, None] * (shifted * inside)]
    ppermute x3, waiting for transfers between devices: 0.15 us -> 1.75 us  [padded(): lax.ppermute(head, axis, [((i + 1) % count, i) for i in range(ends)])]
  transfers between devices with their start and end apart: 6 -> 21, of which waited for: 1 -> 15; matrix products, arithmetic and copies ran while one was open for 9% -> 9% of each run, Pallas kernels for 0% -> 0%
where the time goes in v1:
time: 116 us; the launch traced here: 115 us
  starting transfers between devices  42.5 us (37%)
  blocking collectives  37.1 us (32%)
  other arithmetic  15.6 us (13%)
  waiting for transfers between devices  13.8 us (12%)
  local copies, waits for them, and re-layouts  4.87 us (4%)
    pmax x1, blocking collectives, on_device(): best_over_a = lax.pmax(jnp.max(score, axis=(0, 1)), 'arow')  37.1 us
    ppermute x7, starting transfers between devices, routes_all_group(): lax.ppermute(local_next[-1] if local_next else u_in, mesh_name, slots)  31.6 us
    ppermute x8, waiting for transfers between devices, routes_all_group(): x_next.append(lax.ppermute(x_next[-1] if x_next else u_in, mesh_name, made))  8.8 us
    ppermute x3, starting transfers between devices, padded(): lax.ppermute(tail, axis, [(i, (i + 1) % count) for i in range(ends)])  6.42 us
    convert_element_type x6, other arithmetic, conv_a(): row_slab = lax.slice_in_dim(values, row_tap, row_tap + out_rows, axis=val...  5.23 us
    reduce_sum x2, other arithmetic, second_layer(): summed = jnp.sum(conv_b(spread, kern_b, map_width), axis=0)  4.84 us
    add x4, other arithmetic, conv_a(): result + kernel[..., row_tap, col_tap][..., None, None, None] * shifted_z...  4.64 us
    ppermute x3, starting transfers between devices, padded(): lax.ppermute(head, axis, [((i + 1) % count, i) for i in range(ends)])  4.06 us
  transfers between devices with their start and end apart: 21, of which 15 were waited for; matrix products, arithmetic and copies ran while one was open for 9% of the time, Pallas kernels for 0%

profile of v1, /device:TPU:0, one launch (start us, length us, event | category | flops | bytes accessed | tf_op | source)
XLA Modules:
  0.0 115.1 jit_solution(9090903741477587028)
XLA Ops:
  0.5 5.0 %collective-permute-start.8 = (bf16[1,32,256]{2,1,0:T(8,128)(2,1)}, bf16[1,32,256]{2,1,0:T(8,128)(2,1)S(1)}, u32[]{:S(2)}, u32[]{:S(2)}) collective-permute-start(bf16[1,32,256]{2,1,0:T(8,128)(2,1)} %param.9), channel_id=1, source_target_pairs={{1,0},{2,1},{3,2},{4,3},{5,4},{6,5},{7,6},{8,7},{9,8},{10,9},{11,1... | collective-permute-start | bytes 49160 | tf_op jit(solution)/shard_map/ppermute | solution.py:104
  5.5 0.8 slice_bitcast_fusion.34
  6.3 0.7 collective-permute-done
  7.1 0.8 slice_bitcast_fusion.35
  7.9 5.0 %collective-permute-done.1 = bf16[1,32,256]{2,1,0:T(8,128)(2,1)S(1)} collective-permute-done((bf16[1,32,256]{2,1,0:T(8,128)(2,1)S(1)}, bf16[1,32,256]{2,1,0:T(8,128)(2,1)S(1)}, u32[]{:S(2)}, u32[]{:S(2)}) %collective-permute-start.1) | collective-permute-done | bytes 16416 | tf_op jit(solution)/shard_map/ppermute | solution.py:101
  12.9 0.8 slice_bitcast_fusion.36
  13.8 4.5 %collective-permute-start.9 = (bf16[1,32,256]{2,1,0:T(8,128)(2,1)S(1)}, bf16[1,32,256]{2,1,0:T(8,128)(2,1)S(1)}, u32[]{:S(2)}, u32[]{:S(2)}) collective-permute-start(bf16[1,32,256]{2,1,0:T(8,128)(2,1)S(1)} %collective-permute-done.8), channel_id=1, source_target_pairs={{1,0},{2,1},{3,2},{4,3},{5,4},{6,5},{7,6},{8,7},{9,8},{10,9},{11,1... | collective-permute-start | bytes 49160 | tf_op jit(solution)/shard_map/ppermute | solution.py:104
  18.8 0.8 slice_bitcast_fusion.37
  19.7 4.4 %collective-permute-start.10 = (bf16[1,32,256]{2,1,0:T(8,128)(2,1)S(1)}, bf16[1,32,256]{2,1,0:T(8,128)(2,1)S(1)}, u32[]{:S(2)}, u32[]{:S(2)}) collective-permute-start(bf16[1,32,256]{2,1,0:T(8,128)(2,1)S(1)} %collective-permute-done.9), channel_id=1, source_target_pairs={{1,0},{2,1},{3,2},{4,3},{5,4},{6,5},{7,6},{8,7},{9,8},{10,9},{11,1... | collective-permute-start | bytes 49160 | tf_op jit(solution)/shard_map/ppermute | solution.py:104
  24.7 0.9 collective-permute-done.10
  25.6 4.4 %collective-permute-start.11 = (bf16[1,32,256]{2,1,0:T(8,128)(2,1)S(1)}, bf16[1,32,256]{2,1,0:T(8,128)(2,1)S(1)}, u32[]{:S(2)}, u32[]{:S(2)}) collective-permute-start(bf16[1,32,256]{2,1,0:T(8,128)(2,1)S(1)} %collective-permute-done.10), channel_id=1, source_target_pairs={{1,0},{2,1},{3,2},{4,3},{5,4},{6,5},{7,6},{8,7},{9,8},{10,9},{11,1... | collective-permute-start | bytes 49160 | tf_op jit(solution)/shard_map/ppermute | solution.py:104
  30.5 0.9 collective-permute-done.11
  31.4 4.4 %collective-permute-start.12 = (bf16[1,32,256]{2,1,0:T(8,128)(2,1)S(1)}, bf16[1,32,256]{2,1,0:T(8,128)(2,1)S(1)}, u32[]{:S(2)}, u32[]{:S(2)}) collective-permute-start(bf16[1,32,256]{2,1,0:T(8,128)(2,1)S(1)} %collective-permute-done.11), channel_id=1, source_target_pairs={{1,0},{2,1},{3,2},{4,3},{5,4},{6,5},{7,6},{8,7},{9,8},{10,9},{11,1... | collective-permute-start | bytes 49160 | tf_op jit(solution)/shard_map/ppermute | solution.py:104
  36.4 0.9 collective-permute-done.12
  37.3 4.4 %collective-permute-start.13 = (bf16[1,32,256]{2,1,0:T(8,128)(2,1)S(1)}, bf16[1,32,256]{2,1,0:T(8,128)(2,1)S(1)}, u32[]{:S(2)}, u32[]{:S(2)}) collective-permute-start(bf16[1,32,256]{2,1,0:T(8,128)(2,1)S(1)} %collective-permute-done.12), channel_id=1, source_target_pairs={{1,0},{2,1},{3,2},{4,3},{5,4},{6,5},{7,6},{8,7},{9,8},{10,9},{11,1... | collective-permute-start | bytes 49160 | tf_op jit(solution)/shard_map/ppermute | solution.py:104
  43.2 4.4 %collective-permute-start.14 = (bf16[1,32,256]{2,1,0:T(8,128)(2,1)S(1)}, bf16[1,32,256]{2,1,0:T(8,128)(2,1)S(1)}, u32[]{:S(2)}, u32[]{:S(2)}) collective-permute-start(bf16[1,32,256]{2,1,0:T(8,128)(2,1)S(1)} %collective-permute-done.13), channel_id=1, source_target_pairs={{1,0},{2,1},{3,2},{4,3},{5,4},{6,5},{7,6},{8,7},{9,8},{10,9},{11,1... | collective-permute-start | bytes 49160 | tf_op jit(solution)/shard_map/ppermute | solution.py:104
  48.2 0.7 constant_dynamic-update-slice_fusion.7
  49.8 1.3 %collective-permute-start.15 = (bf16[1,32,512]{2,1,0:T(8,128)(2,1)S(1)}, bf16[1,32,512]{2,1,0:T(8,128)(2,1)S(1)}, u32[]{:S(2)}, u32[]{:S(2)}) collective-permute-start(bf16[1,32,512]{2,1,0:T(8,128)(2,1)S(1)} %get-tuple-element.28), channel_id=1, source_target_pairs={{0,1},{1,2},{2,3},{3,4},{4,5},{5,6},{6,7},{7,8},{8,9},{9,10},{10,1... | collective-permute-start | bytes 98312 | tf_op jit(solution)/shard_map/ppermute | solution.py:23
  51.1 1.3 %collective-permute-start.16 = (bf16[1,32,512]{2,1,0:T(8,128)(2,1)S(1)}, bf16[1,32,512]{2,1,0:T(8,128)(2,1)S(1)}, u32[]{:S(2)}, u32[]{:S(2)}) collective-permute-start(bf16[1,32,512]{2,1,0:T(8,128)(2,1)S(1)} %get-tuple-element.29), channel_id=1, source_target_pairs={{1,0},{2,1},{3,2},{4,3},{5,4},{6,5},{7,6},{8,7},{9,8},{10,9},{11,1... | collective-permute-start | bytes 98312 | tf_op jit(solution)/shard_map/ppermute | solution.py:25
  52.5 1.7 %collective-permute-done.16 = bf16[1,32,512]{2,1,0:T(8,128)(2,1)S(1)} collective-permute-done((bf16[1,32,512]{2,1,0:T(8,128)(2,1)S(1)}, bf16[1,32,512]{2,1,0:T(8,128)(2,1)S(1)}, u32[]{:S(2)}, u32[]{:S(2)}) %collective-permute-start.16) | collective-permute-done | bytes 32800 | tf_op jit(solution)/shard_map/ppermute | solution.py:25
  55.8 2.5 %fusion.152 = (f32[8,2,32,512]{3,2,1,0:T(8,128)S(1)}, bf16[8,2,32,512]{3,2,1,0:T(8,128)(2,1)S(1)}) fusion(f32[8]{0:T(128)S(1)} %copy-done.1, f32[8,2,32,512]{3,2,1,0:T(8,128)S(1)} %multiply_add_fusion.1, f32[8]{0:T(128)S(1)} %get-tuple-element.64, f32[8]{0:T(128)S(1)} %get-tuple-element.65, f32[8]{0:T(128)S(1)} %get-tuple-element.58, ...), kind=kLoop, calls=%fused_computation.279 | loop fusion | flops 7864320 | bytes 2627904 | tf_op jit(solution)/shard_map/convert_element_type | solution.py:50
  58.3 2.1 %collective-permute-start.17 = (bf16[8,1,32,512]{3,2,1,0:T(8,128)(2,1)S(1)}, bf16[8,1,32,512]{3,2,1,0:T(8,128)(2,1)S(1)}, u32[]{:S(2)}, u32[]{:S(2)}) collective-permute-start(bf16[8,1,32,512]{3,2,1,0:T(8,128)(2,1)S(1)} %get-tuple-element.15), channel_id=1, source_target_pairs={{0,1},{1,2},{2,3},{3,4},{4,5},{5,6},{6,7},{7,8},{8,9},{9,10},{10,1... | collective-permute-start | bytes 786440 | tf_op jit(solution)/shard_map/ppermute | solution.py:23
  60.4 1.3 %collective-permute-start.18 = (bf16[8,1,32,512]{3,2,1,0:T(8,128)(2,1)S(1)}, bf16[8,1,32,512]{3,2,1,0:T(8,128)(2,1)S(1)}, u32[]{:S(2)}, u32[]{:S(2)}) collective-permute-start(bf16[8,1,32,512]{3,2,1,0:T(8,128)(2,1)S(1)} %get-tuple-element.14), channel_id=1, source_target_pairs={{1,0},{2,1},{3,2},{4,3},{5,4},{6,5},{7,6},{8,7},{9,8},{10,9},{11,1... | collective-permute-start | bytes 786440 | tf_op jit(solution)/shard_map/ppermute | solution.py:25
  61.7 2.5 %fusion.154 = (f32[8,2,32,512]{3,2,1,0:T(8,128)S(1)}, bf16[8,2,32,512]{3,2,1,0:T(8,128)(2,1)S(1)}) fusion(f32[8]{0:T(128)S(1)} %copy-done.1, f32[8,2,32,512]{3,2,1,0:T(8,128)S(1)} %multiply_add_fusion, f32[8]{0:T(128)S(1)} %get-tuple-element.55, f32[8]{0:T(128)S(1)} %get-tuple-element.56, f32[8]{0:T(128)S(1)} %get-tuple-element.49, ...), kind=kLoop, calls=%fused_computation.280 | loop fusion | flops 7864320 | bytes 2627904 | tf_op jit(solution)/shard_map/convert_element_type | solution.py:50
  64.2 3.0 %collective-permute-start.19 = (bf16[8,1,32,512]{3,2,1,0:T(8,128)(2,1)S(1)}, bf16[8,1,32,512]{3,2,1,0:T(8,128)(2,1)S(1)}, u32[]{:S(2)}, u32[]{:S(2)}) collective-permute-start(bf16[8,1,32,512]{3,2,1,0:T(8,128)(2,1)S(1)} %get-tuple-element.19), channel_id=1, source_target_pairs={{0,1},{1,2},{2,3},{3,4},{4,5},{5,6},{6,7},{7,8},{8,9},{9,10},{10,1... | collective-permute-start | bytes 786440 | tf_op jit(solution)/shard_map/ppermute | solution.py:23
  67.2 1.5 %collective-permute-start.20 = (bf16[8,1,32,512]{3,2,1,0:T(8,128)(2,1)S(1)}, bf16[8,1,32,512]{3,2,1,0:T(8,128)(2,1)S(1)}, u32[]{:S(2)}, u32[]{:S(2)}) collective-permute-start(bf16[8,1,32,512]{3,2,1,0:T(8,128)(2,1)S(1)} %get-tuple-element.18), channel_id=1, source_target_pairs={{1,0},{2,1},{3,2},{4,3},{5,4},{6,5},{7,6},{8,7},{9,8},{10,9},{11,1... | collective-permute-start | bytes 786440 | tf_op jit(solution)/shard_map/ppermute | solution.py:25
  68.9 1.6 %fusion.35 = f32[8,2,32,512]{3,2,1,0:T(8,128)S(1)} fusion(f32[8,2,32,512]{3,2,1,0:T(8,128)S(1)} %get-tuple-element.13, f32[8,2,32,512]{3,2,1,0:T(8,128)S(1)} %get-tuple-element.8, f32[8,2,32,512]{3,2,1,0:T(8,128)S(1)} %get-tuple-element.12, f32[8]{0:T(128)S(1)} %get-tuple-element.37, f32[8]{0:T(128)S(1)} %get-tuple-element.38, f32[8]{0:T(128)S(1)} %get-tuple-element.31, ...), kind=kLoop, calls=%fused_computation.81 | loop fusion | flops 4456448 | bytes 4194592 | tf_op jit(solution)/shard_map/add | solution.py:52
  70.5 2.4 %fusion.132 = f32[2,32,512]{2,1,0:T(8,128)S(1)} fusion(f32[8,2,32,512]{3,2,1,0:T(8,128)S(1)} %fusion.35, f32[8]{0:T(128)S(1)} %get-tuple-element.46, f32[8]{0:T(128)S(1)} %get-tuple-element.47, f32[8]{0:T(128)S(1)} %get-tuple-element.40, f32[8]{0:T(128)S(1)} %get-tuple-element.41, f32[8]{0:T(128)S(1)} %get-tuple-element.42, f32[8]{0:T(128)S(1)} %get-tuple-element.43, ...), kind=kLoop, calls=%fused_computation.180 | loop fusion | flops 7045120 | bytes 1186080 | tf_op jit(solution)/shard_map/reduce_sum | solution.py:84
  73.1 1.6 %fusion.99 = f32[8,2,32,512]{3,2,1,0:T(8,128)S(1)} fusion(f32[8,2,32,512]{3,2,1,0:T(8,128)S(1)} %get-tuple-element.17, f32[8,2,32,512]{3,2,1,0:T(8,128)S(1)} %get-tuple-element.10, f32[8,2,32,512]{3,2,1,0:T(8,128)S(1)} %get-tuple-element.16, f32[8]{0:T(128)S(1)} %get-tuple-element.46, f32[8]{0:T(128)S(1)} %get-tuple-element.47, f32[8]{0:T(128)S(1)} %get-tuple-element.40, ...), kind=kLoop, calls=%fused_computation.145 | loop fusion | flops 4456448 | bytes 4194592 | tf_op jit(solution)/shard_map/add | solution.py:52
  74.7 2.4 %fusion.131 = f32[2,32,512]{2,1,0:T(8,128)S(1)} fusion(f32[8,2,32,512]{3,2,1,0:T(8,128)S(1)} %fusion.99, f32[8]{0:T(128)S(1)} %get-tuple-element.37, f32[8]{0:T(128)S(1)} %get-tuple-element.38, f32[8]{0:T(128)S(1)} %get-tuple-element.31, f32[8]{0:T(128)S(1)} %get-tuple-element.32, f32[8]{0:T(128)S(1)} %get-tuple-element.33, f32[8]{0:T(128)S(1)} %get-tuple-element.34, ...), kind=kLoop, calls=%fused_computation.179 | loop fusion | flops 7045120 | bytes 1186080 | tf_op jit(solution)/shard_map/reduce_sum | solution.py:84
  77.2 37.1 %pmax.7 = f32[512]{0:T(512)S(1)} all-reduce(f32[512]{0:T(512)S(1)} %get-tuple-element.5), channel_id=1, replica_groups=mesh['groups'=2,'arow'=16] {'arow'}, use_global_device_ids=true, to_apply=%region_3.4 | all-reduce | flops 512 | bytes 4096 | tf_op jit(solution)/shard_map/pmax | solution.py:131
  114.4 0.7 fusion.137
  (62 shorter events, 6.9 us)
Async XLA Ops:
  0.0 49.6 %copy-start = (bf16[2,32,256]{2,1,0:T(8,128)(2,1)S(1)}, bf16[2,32,256]{2,1,0:T(8,128)(2,1)}, u32[]{:S(2)}) copy-start(bf16[2,32,256]{2,1,0:T(8,128)(2,1)} %param.8) | copy-start | bytes 98308
  0.0 7.0 %collective-permute-start = (bf16[1,32,256]{2,1,0:T(8,128)(2,1)}, bf16[1,32,256]{2,1,0:T(8,128)(2,1)S(1)}, u32[]{:S(2)}, u32[]{:S(2)}) collective-permute-start(bf16[1,32,256]{2,1,0:T(8,128)(2,1)} %param.9), channel_id=1, source_target_pairs={{0,1},{1,2},{2,3},{3,4},{4,5},{5,6},{6,7},{7,8},{8,9},{9,10},{10,1... | collective-permute-start | bytes 49160 | tf_op jit(solution)/shard_map/ppermute | solution.py:101
  0.5 13.3 %collective-permute-start.8 = (bf16[1,32,256]{2,1,0:T(8,128)(2,1)}, bf16[1,32,256]{2,1,0:T(8,128)(2,1)S(1)}, u32[]{:S(2)}, u32[]{:S(2)}) collective-permute-start(bf16[1,32,256]{2,1,0:T(8,128)(2,1)} %param.9), channel_id=1, source_target_pairs={{1,0},{2,1},{3,2},{4,3},{5,4},{6,5},{7,6},{8,7},{9,8},{10,9},{11,1... | collective-permute-start | bytes 49160 | tf_op jit(solution)/shard_map/ppermute | solution.py:104
  7.1 5.9 %collective-permute-start.1 = (bf16[1,32,256]{2,1,0:T(8,128)(2,1)S(1)}, bf16[1,32,256]{2,1,0:T(8,128)(2,1)S(1)}, u32[]{:S(2)}, u32[]{:S(2)}) collective-permute-start(bf16[1,32,256]{2,1,0:T(8,128)(2,1)S(1)} %collective-permute-done), channel_id=1, source_target_pairs={{0,1},{1,2},{2,3},{3,4},{4,5},{5,6},{6,7},{7,8},{8,9},{9,10},{10,1... | collective-permute-start | bytes 49160 | tf_op jit(solution)/shard_map/ppermute | solution.py:101
  12.9 5.9 %collective-permute-start.2 = (bf16[1,32,256]{2,1,0:T(8,128)(2,1)S(1)}, bf16[1,32,256]{2,1,0:T(8,128)(2,1)S(1)}, u32[]{:S(2)}, u32[]{:S(2)}) collective-permute-start(bf16[1,32,256]{2,1,0:T(8,128)(2,1)S(1)} %collective-permute-done.1), channel_id=1, source_target_pairs={{0,1},{1,2},{2,3},{3,4},{4,5},{5,6},{6,7},{7,8},{8,9},{9,10},{10,1... | collective-permute-start | bytes 49160 | tf_op jit(solution)/shard_map/ppermute | solution.py:101
  13.8 5.9 %collective-permute-start.9 = (bf16[1,32,256]{2,1,0:T(8,128)(2,1)S(1)}, bf16[1,32,256]{2,1,0:T(8,128)(2,1)S(1)}, u32[]{:S(2)}, u32[]{:S(2)}) collective-permute-start(bf16[1,32,256]{2,1,0:T(8,128)(2,1)S(1)} %collective-permute-done.8), channel_id=1, source_target_pairs={{1,0},{2,1},{3,2},{4,3},{5,4},{6,5},{7,6},{8,7},{9,8},{10,9},{11,1... | collective-permute-start | bytes 49160 | tf_op jit(solution)/shard_map/ppermute | solution.py:104
  18.8 5.9 %collective-permute-start.3 = (bf16[1,32,256]{2,1,0:T(8,128)(2,1)S(1)}, bf16[1,32,256]{2,1,0:T(8,128)(2,1)S(1)}, u32[]{:S(2)}, u32[]{:S(2)}) collective-permute-start(bf16[1,32,256]{2,1,0:T(8,128)(2,1)S(1)} %collective-permute-done.2), channel_id=1, source_target_pairs={{0,1},{1,2},{2,3},{3,4},{4,5},{5,6},{6,7},{7,8},{8,9},{9,10},{10,1... | collective-permute-start | bytes 49160 | tf_op jit(solution)/shard_map/ppermute | solution.py:101
  19.7 5.9 %collective-permute-start.10 = (bf16[1,32,256]{2,1,0:T(8,128)(2,1)S(1)}, bf16[1,32,256]{2,1,0:T(8,128)(2,1)S(1)}, u32[]{:S(2)}, u32[]{:S(2)}) collective-permute-start(bf16[1,32,256]{2,1,0:T(8,128)(2,1)S(1)} %collective-permute-done.9), channel_id=1, source_target_pairs={{1,0},{2,1},{3,2},{4,3},{5,4},{6,5},{7,6},{8,7},{9,8},{10,9},{11,1... | collective-permute-start | bytes 49160 | tf_op jit(solution)/shard_map/ppermute | solution.py:104
  24.6 5.9 %collective-permute-start.4 = (bf16[1,32,256]{2,1,0:T(8,128)(2,1)S(1)}, bf16[1,32,256]{2,1,0:T(8,128)(2,1)S(1)}, u32[]{:S(2)}, u32[]{:S(2)}) collective-permute-start(bf16[1,32,256]{2,1,0:T(8,128)(2,1)S(1)} %collective-permute-done.3), channel_id=1, source_target_pairs={{0,1},{1,2},{2,3},{3,4},{4,5},{5,6},{6,7},{7,8},{8,9},{9,10},{10,1... | collective-permute-start | bytes 49160 | tf_op jit(solution)/shard_map/ppermute | solution.py:101
  25.6 5.9 %collective-permute-start.11 = (bf16[1,32,256]{2,1,0:T(8,128)(2,1)S(1)}, bf16[1,32,256]{2,1,0:T(8,128)(2,1)S(1)}, u32[]{:S(2)}, u32[]{:S(2)}) collective-permute-start(bf16[1,32,256]{2,1,0:T(8,128)(2,1)S(1)} %collective-permute-done.10), channel_id=1, source_target_pairs={{1,0},{2,1},{3,2},{4,3},{5,4},{6,5},{7,6},{8,7},{9,8},{10,9},{11,1... | collective-permute-start | bytes 49160 | tf_op jit(solution)/shard_map/ppermute | solution.py:104
  30.5 5.9 %collective-permute-start.5 = (bf16[1,32,256]{2,1,0:T(8,128)(2,1)S(1)}, bf16[1,32,256]{2,1,0:T(8,128)(2,1)S(1)}, u32[]{:S(2)}, u32[]{:S(2)}) collective-permute-start(bf16[1,32,256]{2,1,0:T(8,128)(2,1)S(1)} %collective-permute-done.4), channel_id=1, source_target_pairs={{0,1},{1,2},{2,3},{3,4},{4,5},{5,6},{6,7},{7,8},{8,9},{9,10},{10,1... | collective-permute-start | bytes 49160 | tf_op jit(solution)/shard_map/ppermute | solution.py:101
  31.4 5.9 %collective-permute-start.12 = (bf16[1,32,256]{2,1,0:T(8,128)(2,1)S(1)}, bf16[1,32,256]{2,1,0:T(8,128)(2,1)S(1)}, u32[]{:S(2)}, u32[]{:S(2)}) collective-permute-start(bf16[1,32,256]{2,1,0:T(8,128)(2,1)S(1)} %collective-permute-done.11), channel_id=1, source_target_pairs={{1,0},{2,1},{3,2},{4,3},{5,4},{6,5},{7,6},{8,7},{9,8},{10,9},{11,1... | collective-permute-start | bytes 49160 | tf_op jit(solution)/shard_map/ppermute | solution.py:104
  36.4 5.9 %collective-permute-start.6 = (bf16[1,32,256]{2,1,0:T(8,128)(2,1)S(1)}, bf16[1,32,256]{2,1,0:T(8,128)(2,1)S(1)}, u32[]{:S(2)}, u32[]{:S(2)}) collective-permute-start(bf16[1,32,256]{2,1,0:T(8,128)(2,1)S(1)} %collective-permute-done.5), channel_id=1, source_target_pairs={{0,1},{1,2},{2,3},{3,4},{4,5},{5,6},{6,7},{7,8},{8,9},{9,10},{10,1... | collective-permute-start | bytes 49160 | tf_op jit(solution)/shard_map/ppermute | solution.py:101
  37.3 5.9 %collective-permute-start.13 = (bf16[1,32,256]{2,1,0:T(8,128)(2,1)S(1)}, bf16[1,32,256]{2,1,0:T(8,128)(2,1)S(1)}, u32[]{:S(2)}, u32[]{:S(2)}) collective-permute-start(bf16[1,32,256]{2,1,0:T(8,128)(2,1)S(1)} %collective-permute-done.12), channel_id=1, source_target_pairs={{1,0},{2,1},{3,2},{4,3},{5,4},{6,5},{7,6},{8,7},{9,8},{10,9},{11,1... | collective-permute-start | bytes 49160 | tf_op jit(solution)/shard_map/ppermute | solution.py:104
  42.2 5.9 %collective-permute-start.7 = (bf16[1,32,256]{2,1,0:T(8,128)(2,1)S(1)}, bf16[1,32,256]{2,1,0:T(8,128)(2,1)S(1)}, u32[]{:S(2)}, u32[]{:S(2)}) collective-permute-start(bf16[1,32,256]{2,1,0:T(8,128)(2,1)S(1)} %collective-permute-done.6), channel_id=1, source_target_pairs={{0,1},{1,2},{2,3},{3,4},{4,5},{5,6},{6,7},{7,8},{8,9},{9,10},{10,1... | collective-permute-start | bytes 49160 | tf_op jit(solution)/shard_map/ppermute | solution.py:101
  43.2 5.9 %collective-permute-start.14 = (bf16[1,32,256]{2,1,0:T(8,128)(2,1)S(1)}, bf16[1,32,256]{2,1,0:T(8,128)(2,1)S(1)}, u32[]{:S(2)}, u32[]{:S(2)}) collective-permute-start(bf16[1,32,256]{2,1,0:T(8,128)(2,1)S(1)} %collective-permute-done.13), channel_id=1, source_target_pairs={{1,0},{2,1},{3,2},{4,3},{5,4},{6,5},{7,6},{8,7},{9,8},{10,9},{11,1... | collective-permute-start | bytes 49160 | tf_op jit(solution)/shard_map/ppermute | solution.py:104
  49.8 2.7 %collective-permute-start.15 = (bf16[1,32,512]{2,1,0:T(8,128)(2,1)S(1)}, bf16[1,32,512]{2,1,0:T(8,128)(2,1)S(1)}, u32[]{:S(2)}, u32[]{:S(2)}) collective-permute-start(bf16[1,32,512]{2,1,0:T(8,128)(2,1)S(1)} %get-tuple-element.28), channel_id=1, source_target_pairs={{0,1},{1,2},{2,3},{3,4},{4,5},{5,6},{6,7},{7,8},{8,9},{9,10},{10,1... | collective-permute-start | bytes 98312 | tf_op jit(solution)/shard_map/ppermute | solution.py:23
  51.1 3.1 %collective-permute-start.16 = (bf16[1,32,512]{2,1,0:T(8,128)(2,1)S(1)}, bf16[1,32,512]{2,1,0:T(8,128)(2,1)S(1)}, u32[]{:S(2)}, u32[]{:S(2)}) collective-permute-start(bf16[1,32,512]{2,1,0:T(8,128)(2,1)S(1)} %get-tuple-element.29), channel_id=1, source_target_pairs={{1,0},{2,1},{3,2},{4,3},{5,4},{6,5},{7,6},{8,7},{9,8},{10,9},{11,1... | collective-permute-start | bytes 98312 | tf_op jit(solution)/shard_map/ppermute | solution.py:25
  55.0 0.7 copy-start.1
  58.3 10.4 %collective-permute-start.17 = (bf16[8,1,32,512]{3,2,1,0:T(8,128)(2,1)S(1)}, bf16[8,1,32,512]{3,2,1,0:T(8,128)(2,1)S(1)}, u32[]{:S(2)}, u32[]{:S(2)}) collective-permute-start(bf16[8,1,32,512]{3,2,1,0:T(8,128)(2,1)S(1)} %get-tuple-element.15), channel_id=1, source_target_pairs={{0,1},{1,2},{2,3},{3,4},{4,5},{5,6},{6,7},{7,8},{8,9},{9,10},{10,1... | collective-permute-start | bytes 786440 | tf_op jit(solution)/shard_map/ppermute | solution.py:23
  60.4 8.4 %collective-permute-start.18 = (bf16[8,1,32,512]{3,2,1,0:T(8,128)(2,1)S(1)}, bf16[8,1,32,512]{3,2,1,0:T(8,128)(2,1)S(1)}, u32[]{:S(2)}, u32[]{:S(2)}) collective-permute-start(bf16[8,1,32,512]{3,2,1,0:T(8,128)(2,1)S(1)} %get-tuple-element.14), channel_id=1, source_target_pairs={{1,0},{2,1},{3,2},{4,3},{5,4},{6,5},{7,6},{8,7},{9,8},{10,9},{11,1... | collective-permute-start | bytes 786440 | tf_op jit(solution)/shard_map/ppermute | solution.py:25
  64.2 8.7 %collective-permute-start.19 = (bf16[8,1,32,512]{3,2,1,0:T(8,128)(2,1)S(1)}, bf16[8,1,32,512]{3,2,1,0:T(8,128)(2,1)S(1)}, u32[]{:S(2)}, u32[]{:S(2)}) collective-permute-start(bf16[8,1,32,512]{3,2,1,0:T(8,128)(2,1)S(1)} %get-tuple-element.19), channel_id=1, source_target_pairs={{0,1},{1,2},{2,3},{3,4},{4,5},{5,6},{6,7},{7,8},{8,9},{9,10},{10,1... | collective-permute-start | bytes 786440 | tf_op jit(solution)/shard_map/ppermute | solution.py:23
  67.2 5.7 %collective-permute-start.20 = (bf16[8,1,32,512]{3,2,1,0:T(8,128)(2,1)S(1)}, bf16[8,1,32,512]{3,2,1,0:T(8,128)(2,1)S(1)}, u32[]{:S(2)}, u32[]{:S(2)}) collective-permute-start(bf16[8,1,32,512]{3,2,1,0:T(8,128)(2,1)S(1)} %get-tuple-element.18), channel_id=1, source_target_pairs={{1,0},{2,1},{3,2},{4,3},{5,4},{6,5},{7,6},{8,7},{9,8},{10,9},{11,1... | collective-permute-start | bytes 786440 | tf_op jit(solution)/shard_map/ppermute | solution.py:25
